TPU v7x, 256 devices: a whole 4x4x8 slice. The times are simulated.
256 devices in a mesh: row: 8 (over x, core), col: 32 (over y, z).
Axes of the slice: x: 4, y: 4, z: 8, core: 2. Of those that a mesh axis runs over, the one named last changes fastest.
Arguments:
- hidden: bfloat16 [128, 8192], P('col', 'row'), may hold values from -6 to 6
- w_gate: bfloat16 [8192, 16384], P('row', 'col'), may hold values from -0.0625 to 0.0625
- w_up: bfloat16 [8192, 16384], P('row', 'col'), may hold values from -0.0625 to 0.0625
- prior: float32 [16384, 16384], P('row', 'col'), may hold values from -1 to 12, as said below
- rhs: float32 [16384, 4096], P('row', 'col'), may hold values from -6 to 6
Outputs:
- factored: float32 [16384, 16384], P('row', 'col')
- right_out: float32 [16384, 4096], P('row', 'col')
Inputs may be any that keep to these rules, and one draw needn't show every extreme that they name: prior is symmetric and positive definite, with smallest eigenvalue 0.1 or more.
All inputs are finite; a program needn't handle non-finite values.
Results may differ from a plain program's by a relative error of at most 0.0003.
Values may be sent and summed in bfloat16 or wider, within the bound.
No kernel may reach another device: no remote copies, remote signals or barrier semaphores. Data moves between devices by JAX's collectives and lax.ppermute only.
A program may use at most 64 MiB of HBM per device.

v0:
```python
import jax
import jax.numpy as jnp
from jax import lax
from jax.sharding import Mesh
from jax.sharding import PartitionSpec as P

P_SIZE = 128
PANELS = 2
COL = ("col_0", "col_1")


DAMP = 0.5


def joined_along(blocks, dim):
    blocks = jnp.moveaxis(blocks, 0, dim)
    lengths = blocks.shape
    return blocks.reshape(*lengths[:dim], lengths[dim] * lengths[dim + 1], *lengths[dim + 2 :])


def copy_for_each(shard, axis):
    peers = lax.axis_size(axis)
    return lax.all_to_all(
        jnp.broadcast_to(shard[None], (peers, *shard.shape)), axis, 0, 0, tiled=True
    )


def gathered_copies(shard, axis, dim):
    return joined_along(copy_for_each(shard, axis), dim)


def side_by_side(arrays, axis, dim, along):
    both = jnp.concatenate(arrays, axis=along)
    result, at, finished = (lax.psum_scatter(both, axis, scatter_dimension=dim, tiled=True), 0, [])
    for a in arrays:
        finished.append(lax.slice_in_dim(result, at, at + a.shape[along], axis=along))
        at += a.shape[along]
    return tuple(finished)


def spread(shard, axes, root):
    shard = jnp.where(lax.axis_index(axes) == root, shard, jnp.zeros_like(shard))
    for axis in axes:
        shard = lax.psum(shard, axis)
    return shard


def broadcast(shard, axis, root):
    return lax.dynamic_index_in_dim(lax.all_gather(shard, axis), root, 0, keepdims=False)


def local(hidden, w_gate, w_up, prior, rhs):
    rows_count = lax.axis_size("row")
    cols_count = lax.axis_size(COL)
    row_id = lax.axis_index("row")
    col_id = lax.axis_index(COL)
    ratio = cols_count // rows_count
    height, width = prior.shape
    tokens = gathered_copies(hidden, COL, 0)
    gate_part = jnp.dot(tokens, w_gate, preferred_element_type=jnp.float32)
    up_part = jnp.dot(tokens, w_up, preferred_element_type=jnp.float32)
    gate, upward = side_by_side((gate_part, up_part), "row", 0, 1)
    keys = gathered_copies(jax.nn.silu(gate) * upward, "row", 0)
    samples = keys.shape[0]
    regrouped = lax.all_to_all(keys, COL, split_axis=0, concat_axis=1, tiled=True)
    own_part = lax.dynamic_slice_in_dim(regrouped, row_id * height, height, 1)
    row_keys = gathered_copies(own_part, COL, 0)
    row_global = row_id * height + lax.iota(jnp.int32, height)
    col_global = col_id * width + lax.iota(jnp.int32, width)
    outer = lax.dot_general(
        row_keys,
        keys,
        (((0,), (0,)), ((), ())),
        precision=lax.Precision.HIGHEST,
        preferred_element_type=jnp.float32,
    )
    work = prior + outer / samples
    work = work + jnp.where(row_global[:, None] == col_global[None, :], DAMP, 0.0).astype(
        jnp.float32
    )
    right = rhs
    offsets = lax.iota(jnp.int32, P_SIZE)
    for panel in range(PANELS):
        start = panel * P_SIZE
        stop = start + P_SIZE
        column = spread(work[:, start:stop], COL, 0)
        pivot = jnp.linalg.cholesky(broadcast(column[start:stop], "row", 0))
        solved = jax.scipy.linalg.solve_triangular(pivot, column.T, lower=True).T
        placed = jnp.zeros_like(solved).at[start:stop].set(pivot)
        in_pivot = (row_global >= start) & (row_global < stop)
        beyond = row_global >= stop
        factor_cols = jnp.where(in_pivot[:, None], placed, jnp.where(beyond[:, None], solved, 0.0))
        matching = lax.dynamic_slice_in_dim(factor_cols, col_id % ratio * width, width, 0)
        across = broadcast(matching, "row", col_id // ratio)
        lower_rows = jnp.where(beyond[:, None], factor_cols, 0.0)
        upper_cols = jnp.where((col_global >= stop)[:, None], across, 0.0)
        work = work - lax.dot_general(
            lower_rows,
            upper_cols,
            (((1,), (1,)), ((), ())),
            precision=lax.Precision.HIGHEST,
            preferred_element_type=jnp.float32,
        )
        solution = jax.scipy.linalg.solve_triangular(
            factor_cols[start:stop], right[start:stop], lower=True
        )
        solution = broadcast(solution, "row", 0)
        right = right - jnp.dot(
            lower_rows,
            solution,
            precision=lax.Precision.HIGHEST,
            preferred_element_type=jnp.float32,
        )
        right = right.at[start:stop].set(jnp.where(row_id == 0, solution, right[start:stop]))
        keep_factor = (row_global[:, None] >= start + offsets[None, :]) & (col_id == 0)
        work = work.at[:, start:stop].set(jnp.where(keep_factor, factor_cols, work[:, start:stop]))
    return (work, right)


def solution(mesh):
    finer = Mesh(mesh.devices.reshape(mesh.shape["row"], 4, 8), ("row", "col_0", "col_1"))
    placed = (P(COL, "row"), P("row", COL), P("row", COL), P("row", COL), P("row", COL))
    return jax.shard_map(
        local,
        mesh=finer,
        in_specs=placed,
        out_specs=(P("row", COL), P("row", COL)),
        check_vma=False,
    )
```

profile of v0, /device:TPU:4, one launch (start us, length us, event | category | flops | bytes accessed | tf_op | source)
XLA Modules:
  0.0 585.1 jit_solution(16554936312668972503)
XLA Ops:
  8.1 23.7 %all_to_all.34 = bf16[32,4,1024]{2,1,0:T(4,128)(2,1)S(1)} all-to-all(bf16[32,4,1024]{2,1,0:T(4,128)(2,1)S(1)} %broadcast_in_dim.100), channel_id=1, replica_groups=mesh['row'=8,'col_0'=4,'col_1'=8] {'col_0','col_1'}, dimensions={0} | all-to-all | bytes 524288 | tf_op jit(solution)/shard_map/all_to_all | solution.py:23
  34.6 24.4 %reduce-scatter.2.cloned.1.call-done = f32[16,1024]{1,0:T(8,128)} async-done(((f32[128,1024]{1,0:T(8,128)}), f32[16,1024]{1,0:T(8,128)}) %reduce-scatter.2.cloned.1.call-update) | async-done | bytes 65552 | tf_op jit(solution)/shard_map/reduce_scatter | solution.py:34
  59.8 12.3 %all_to_all.35 = f32[8,16,512]{2,1,0:T(8,128)S(1)} all-to-all(f32[8,16,512]{2,1,0:T(8,128)S(1)} %broadcast_in_dim.101), channel_id=1, replica_groups=mesh['row'=8,'col_0'=4,'col_1'=8] {'row'}, dimensions={0} | all-to-all | bytes 524288 | tf_op jit(solution)/shard_map/all_to_all | solution.py:23
  72.9 9.8 %all-to-all-start.2 = ((f32[32,4,512]{2,1,0:T(4,128)}), f32[32,4,512]{2,1,0:T(4,128)S(1)}, u32[]{:S(2)}, u32[]{:S(2)}) async-start(f32[32,4,512]{2,1,0:T(4,128)} %all_to_all.25), calls=%async_computation.3 | async-start | bytes 524288 | tf_op jit(solution)/shard_map/all_to_all | solution.py:65
  82.8 12.5 %all-to-all-done.2 = f32[32,4,512]{2,1,0:T(4,128)S(1)} async-done(((f32[32,4,512]{2,1,0:T(4,128)}), f32[32,4,512]{2,1,0:T(4,128)S(1)}, u32[]{:S(2)}, u32[]{:S(2)}) %all-to-all-start.2) | async-done | bytes 262176 | tf_op jit(solution)/shard_map/all_to_all | solution.py:65
  101.0 28.0 %all-to-all-done.3 = f32[32,4,2048]{2,1,0:T(4,128)S(1)} async-done(((f32[32,4,2048]{2,1,0:T(4,128)}), f32[32,4,2048]{2,1,0:T(4,128)S(1)}, u32[]{:S(2)}, u32[]{:S(2)}) %all-to-all-start.3) | async-done | bytes 1048608 | tf_op jit(solution)/shard_map/all_to_all | solution.py:23
  129.3 5.8 select_add_fusion
  138.3 47.4 %all-reduce.7.cloned.1.call-done = f32[2048,128]{1,0:T(8,128)} async-done(((f32[2048,128]{1,0:T(8,128)}), f32[2048,128]{1,0:T(8,128)}) %all-reduce.7.cloned.1.call-update) | async-done | bytes 1048592 | tf_op jit(solution)/shard_map/psum | solution.py:44
  185.8 79.0 %all-reduce.9.cloned.1.call-done = f32[2048,128]{1,0:T(8,128)} async-done(((f32[2048,128]{1,0:T(8,128)}), f32[2048,128]{1,0:T(8,128)}) %all-reduce.9.cloned.1.call-update) | async-done | bytes 1048592 | tf_op jit(solution)/shard_map/psum | solution.py:44
  265.7 12.1 %all-gather = f32[1024,128]{1,0:T(8,128)S(1)} all-gather(f32[128,128]{1,0:T(8,128)S(1)} %slice.179), channel_id=2, replica_groups=mesh['row'=8,'col_0'=4,'col_1'=8] {'row'}, dimensions={0}, use_global_device_ids=true | all-gather | bytes 589824 | tf_op jit(solution)/shard_map/all_gather | solution.py:49
  278.0 11.7 %cholesky.44 = f32[128,128]{1,0:T(8,128)S(1)} custom-call(f32[128,128]{1,0:T(8,128)S(1)} %copy.8), custom_call_target="Cholesky" | custom-call | tf_op jit(solution)/shard_map/jit(cholesky)/cholesky | solution.py:87
  291.1 9.8 %custom-call.10 = f32[1,128,128]{1,2,0:T(8,128)S(1)} custom-call(f32[1,128,128]{2,1,0:T(8,128)S(1)} %get-tuple-element.79), custom_call_target="InvertDiagBlocksLowerTriangular" | custom-call | tf_op jit(solution)/shard_map/jit(_solve_triangular)/triangular_solve | solution.py:88
  305.6 25.4 %all-gather.9.cloned.1.call-done = f32[4096,128]{1,0:T(8,128)} async-done(((f32[512,128]{1,0:T(8,128)}), f32[4096,128]{1,0:T(8,128)}) %all-gather.9.cloned.1.call-update) | async-done | bytes 2097168 | tf_op jit(solution)/shard_map/all_gather | solution.py:49
  331.0 5.5 convolution_subtract_fusion.1
  340.8 52.3 %all-reduce.11.cloned.1.call-done = f32[2048,128]{1,0:T(8,128)} async-done(((f32[2048,128]{1,0:T(8,128)}), f32[2048,128]{1,0:T(8,128)}) %all-reduce.11.cloned.1.call-update) | async-done | bytes 1048592 | tf_op jit(solution)/shard_map/psum | solution.py:44
  393.2 79.0 %all-reduce.13.cloned.1.call-done = f32[2048,128]{1,0:T(8,128)} async-done(((f32[2048,128]{1,0:T(8,128)}), f32[2048,128]{1,0:T(8,128)}) %all-reduce.13.cloned.1.call-update) | async-done | bytes 1048592 | tf_op jit(solution)/shard_map/psum | solution.py:44
  473.1 12.1 %all-gather.2 = f32[1024,128]{1,0:T(8,128)S(1)} all-gather(f32[128,128]{1,0:T(8,128)S(1)} %slice.183), channel_id=4, replica_groups=mesh['row'=8,'col_0'=4,'col_1'=8] {'row'}, dimensions={0}, use_global_device_ids=true | all-gather | bytes 589824 | tf_op jit(solution)/shard_map/all_gather | solution.py:49
  485.4 11.7 %cholesky.55 = f32[128,128]{1,0:T(8,128)S(1)} custom-call(f32[128,128]{1,0:T(8,128)S(1)} %copy.11), custom_call_target="Cholesky" | custom-call | tf_op jit(solution)/shard_map/jit(cholesky)/cholesky | solution.py:87
  498.5 9.8 %custom-call.11 = f32[1,128,128]{1,2,0:T(8,128)S(1)} custom-call(f32[1,128,128]{2,1,0:T(8,128)S(1)} %get-tuple-element.77), custom_call_target="InvertDiagBlocksLowerTriangular" | custom-call | tf_op jit(solution)/shard_map/jit(_solve_triangular)/triangular_solve | solution.py:88
  513.0 9.8 %custom-call.12 = f32[1,128,128]{1,2,0:T(8,128)S(1)} custom-call(f32[1,128,128]{2,1,0:T(8,128)S(1)} %fusion.32), custom_call_target="InvertDiagBlocksLowerTriangular" | custom-call | tf_op jit(solution)/shard_map/jit(_solve_triangular)/triangular_solve | solution.py:104
  524.0 14.2 %all-gather.4 = f32[1024,128]{1,0:T(8,128)S(1)} all-gather(f32[128,128]{1,0:T(8,128)S(1)} %fusion.34), channel_id=6, replica_groups=mesh['row'=8,'col_0'=4,'col_1'=8] {'row'}, dimensions={0}, use_global_device_ids=true | all-gather | bytes 589824 | tf_op jit(solution)/shard_map/all_gather | solution.py:49
  542.8 9.8 %custom-call.13 = f32[1,128,128]{1,2,0:T(8,128)S(1)} custom-call(f32[1,128,128]{2,1,0:T(8,128)S(1)} %fusion.30), custom_call_target="InvertDiagBlocksLowerTriangular" | custom-call | tf_op jit(solution)/shard_map/jit(_solve_triangular)/triangular_solve | solution.py:104
  553.7 13.1 %all-gather.5 = f32[1024,128]{1,0:T(8,128)S(1)} all-gather(f32[128,128]{1,0:T(8,128)S(1)} %fusion.28), channel_id=7, replica_groups=mesh['row'=8,'col_0'=4,'col_1'=8] {'row'}, dimensions={0}, use_global_device_ids=true | all-gather | bytes 589824 | tf_op jit(solution)/shard_map/all_gather | solution.py:49
  569.2 5.9 %convolution_subtract_fusion = f32[2048,512]{1,0:T(8,128)S(1)} fusion(f32[2048,512]{1,0:T(8,128)} %copy-done.1, f32[2048,128]{1,0:T(8,128)S(1)} %fusion.1, pred[2048]{0:T(1024)(128)(4,1)S(1)} %fusion.44, f32[8,512,128]{2,1,0:T(8,128)} %bitcast.62, s32[]{:T(128)S(6)} %select_n.113, pred[512]{0:T(512)(128)(4,1)S(1)} %fusion.52), kind=kOutput, calls=%fused_computation.1 | convolution fusion | flops 1611988992 | bytes 9701892 | tf_op jit(solution)/shard_map/dot_general | solution.py:97
  (79 shorter events, 45.2 us)
Async XLA Ops:
  7.2 24.7 %copy-start = (bf16[1024,512]{1,0:T(8,128)(2,1)S(1)}, bf16[1024,512]{1,0:T(8,128)(2,1)}, u32[]{:S(2)}) copy-start(bf16[1024,512]{1,0:T(8,128)(2,1)} %param.23) | copy-start | bytes 3145732
  7.2 51.8 %reduce-scatter.2.cloned.1.call-start = ((), (), s32[]{:S(2)}) async-start(), calls=%async_computation.5 | async-start | bytes 589824 | tf_op jit(solution)/shard_map/reduce_scatter | solution.py:34
  72.9 22.3 %all-to-all-start.2 = ((f32[32,4,512]{2,1,0:T(4,128)}), f32[32,4,512]{2,1,0:T(4,128)S(1)}, u32[]{:S(2)}, u32[]{:S(2)}) async-start(f32[32,4,512]{2,1,0:T(4,128)} %all_to_all.25), calls=%async_computation.3 | async-start | bytes 524288 | tf_op jit(solution)/shard_map/all_to_all | solution.py:65
  96.5 32.5 %all-to-all-start.3 = ((f32[32,4,2048]{2,1,0:T(4,128)}), f32[32,4,2048]{2,1,0:T(4,128)S(1)}, u32[]{:S(2)}, u32[]{:S(2)}) async-start(f32[32,4,2048]{2,1,0:T(4,128)} %broadcast_in_dim.102), calls=%async_computation.4 | async-start | bytes 2097152 | tf_op jit(solution)/shard_map/all_to_all | solution.py:23
  100.9 84.8 %all-reduce.7.cloned.1.call-start = ((), (), s32[]{:S(2)}) async-start(), calls=%async_computation.6 | async-start | bytes 2097152 | tf_op jit(solution)/shard_map/psum | solution.py:44
  135.1 2.0 copy-start.2
  138.2 126.6 %all-reduce.9.cloned.1.call-start = ((), (), s32[]{:S(2)}) async-start(), calls=%async_computation.7 | async-start | bytes 2097152 | tf_op jit(solution)/shard_map/psum | solution.py:44
  185.7 145.3 %all-gather.9.cloned.1.call-start = ((), (), s32[]{:S(2)}) async-start(), calls=%async_computation.10 | async-start | bytes 2359296 | tf_op jit(solution)/shard_map/all_gather | solution.py:49
  304.9 88.2 %all-reduce.11.cloned.1.call-start = ((), (), s32[]{:S(2)}) async-start(), calls=%async_computation.8 | async-start | bytes 2097152 | tf_op jit(solution)/shard_map/psum | solution.py:44
  337.6 2.0 copy-start.1
  340.8 131.5 %all-reduce.13.cloned.1.call-start = ((), (), s32[]{:S(2)}) async-start(), calls=%async_computation.9 | async-start | bytes 2097152 | tf_op jit(solution)/shard_map/psum | solution.py:44
  393.1 176.1 %all-gather.11.cloned.1.call-start = ((), (), s32[]{:S(2)}) async-start(), calls=%async_computation.11 | async-start | bytes 2359296 | tf_op jit(solution)/shard_map/all_gather | solution.py:49
  569.2 5.9 %copy-start.4 = (f32[2048,128]{1,0:T(8,128)}, f32[2048,128]{1,0:T(8,128)S(1)}, u32[]{:S(2)}) copy-start(f32[2048,128]{1,0:T(8,128)S(1)} %fusion.27) | copy-start | bytes 3145732
  576.2 2.0 copy-start.3
Sparse Core Ops, SparseCore 0:
  34.7 24.2 reduce-scatter.1
  138.4 47.3 all-reduce.6
  188.1 76.7 all-reduce.8
  305.0 25.9 all-gather.8
  340.9 52.1 all-reduce.10
  395.4 76.7 all-reduce.12
  512.5 27.0 all-gather.10
where the time goes:
time: 589 us; the launch traced here: 585 us
  waiting for transfers between devices  348 us (59%)
  blocking collectives  87.7 us (15%)
  other arithmetic  74.2 us (13%)
  matrix products  33.2 us (6%)
  starting transfers between devices  14.5 us (2%)
  between operations  14.5 us (2%)
  local copies, waits for them, and re-layouts  12.9 us (2%)
    psum x4, waiting for transfers between devices, spread(): shard = lax.psum(shard, axis)  258 us
    all_gather x4, blocking collectives, broadcast(): lax.all_gather(shard, axis)  51.6 us
    all_to_all x2, blocking collectives, copy_for_each(): lax.all_to_all(jnp.broadcast_to(shard[None], (peers, *shard.shape)), axis...  36.1 us
    all_to_all x1, waiting for transfers between devices, copy_for_each(): lax.all_to_all(jnp.broadcast_to(shard[None], (peers, *shard.shape)), axis...  28 us
    all_gather x2, waiting for transfers between devices, broadcast(): lax.all_gather(shard, axis)  25.4 us
    another operation x6, other arithmetic, local(): pivot = jnp.linalg.cholesky(broadcast(column[start:stop], 'row', 0))  24.8 us
    reduce_scatter x1, waiting for transfers between devices, side_by_side(): lax.psum_scatter(both, axis, scatter_dimension=dim, tiled=True)  24.4 us
    another operation x4, other arithmetic, local(): solved = jax.scipy.linalg.solve_triangular(pivot, column.T, lower=True).T  20.9 us
  transfers between devices with their start and end apart: 9, of which 8 were waited for; matrix products, arithmetic and copies ran while one was open for 5% of the time, Pallas kernels for 0%

commit v1 on v0

v1 whole, which is shorter than its diff:
```python
import functools

import jax
import jax.numpy as jnp
from jax import lax
from jax.experimental import pallas as pl
from jax.experimental.pallas import tpu as pltpu
from jax.sharding import Mesh
from jax.sharding import PartitionSpec as P

P_SIZE = 128
WIDE = 256
DAMP = 0.5
ROWS, YS, ZS = 8, 4, 8
COL = ("col_0", "col_1")
ALL = ("row", "col_0", "col_1")
HIGHEST = lax.Precision.HIGHEST
NN = (((1,), (0,)), ((), ()))
TN = (((0,), (0,)), ((), ()))
NT = (((1,), (1,)), ((), ()))


def copies(shard, axis):
    peers = lax.axis_size(axis)
    wide = jnp.broadcast_to(shard[None], (peers, *shard.shape))
    return lax.all_to_all(wide, axis, 0, 0, tiled=True)


def row_tree(x):
    at = lax.axis_index("row")
    for step in (4, 2, 1):
        pairs = [(i, i + step) for i in range(0, ROWS, 2 * step)]
        got = lax.ppermute(x, "row", pairs)
        x = jnp.where(at % (2 * step) == step, got, x)
    return x


def col_tree(x):
    at = lax.axis_index(COL)
    for step in (4, 2, 1):
        pairs = [(i, i + step) for i in range(0, ZS, 2 * step)]
        got = lax.ppermute(x, COL, pairs)
        x = jnp.where(at % (2 * step) == step, got, x)
    for step in (2 * ZS, ZS):
        pairs = [(i + z, i + step + z) for i in range(0, YS * ZS, 2 * step) for z in range(ZS)]
        got = lax.ppermute(x, COL, pairs)
        x = jnp.where(at // ZS * ZS % (2 * step) == step, got, x)
    return x


def to_row_blocks(piece):
    cols = YS * ZS
    pairs = [
        (k * cols + c, (c // YS) * cols + ZS * (c % YS) + k) for k in range(ROWS) for c in range(cols)
    ]
    return lax.ppermute(piece, ALL, pairs)


def gather_row_blocks(piece):
    return copies(copies(to_row_blocks(piece), "col_1"), "col_0")


def split(x):
    high = x.astype(jnp.bfloat16)
    return high, (x - high.astype(jnp.float32)).astype(jnp.bfloat16)


def dot3(a, b, dims):
    ah, al = a
    bh, bl = b
    dot = functools.partial(lax.dot_general, dimension_numbers=dims, preferred_element_type=jnp.float32)
    return dot(ah, bh) + (dot(ah, bl) + dot(al, bh))


def finish_kernel(
    at_ref, prior_ref, rhs_ref, keys_ref, panel_ref, mine_ref, across_ref, first_ref, inverse_ref,
    pivot_ref, solved_ref, out_ref, right_ref,
):
    step = pl.program_id(0)
    row_id = at_ref[0]
    col_id = at_ref[1]
    samples, tall = keys_ref.shape[1:]
    wide = prior_ref.shape[1]
    row_at = (row_id * pl.num_programs(0) + step) * tall
    col_at = col_id * wide
    keys = keys_ref[0]
    scaled = keys * (1.0 / samples)
    first = split(first_ref[...])
    inverse = split(inverse_ref[...])
    scaled_parts = split(scaled)
    crossing = panel_ref[0] + dot3(first, scaled_parts, TN)
    solved = dot3(inverse, split(crossing), NN)
    line = lax.broadcasted_iota(jnp.int32, solved.shape, 0) // P_SIZE
    below = row_at + lax.broadcasted_iota(jnp.int32, solved.shape, 1) >= (line + 1) * P_SIZE
    solved = jnp.where(below, solved, 0.0)
    solved_parts = split(-solved)
    block = prior_ref[...] + dot3(scaled_parts, split(mine_ref[...]), TN)
    block = block + dot3(solved_parts, split(across_ref[...]), TN)
    row = row_at + lax.broadcasted_iota(jnp.int32, block.shape, 0)
    col = col_at + lax.broadcasted_iota(jnp.int32, block.shape, 1)
    out_ref[...] = jnp.where(row == col, block + DAMP, block)
    right_ref[...] = rhs_ref[...] + dot3(solved_parts, split(solved_ref[...]), TN)

    @pl.when(col_id == 0)
    def _():
        own = prior_ref[:, :WIDE] + dot3(scaled_parts, first, TN)
        own = dot3(split(own), inverse, NT)
        row = row_at + lax.broadcasted_iota(jnp.int32, own.shape, 0)
        out_ref[:, :WIDE] = jnp.where(row >= WIDE, own, out_ref[:, :WIDE])

    @pl.when(row_at == 0)
    def _():
        right_ref[:WIDE, :] = solved_ref[...]

        @pl.when(col_id == 0)
        def _():
            row = lax.broadcasted_iota(jnp.int32, (WIDE, WIDE), 0)
            col = lax.broadcasted_iota(jnp.int32, (WIDE, WIDE), 1)
            out_ref[:WIDE, :WIDE] = jnp.where(row >= col, pivot_ref[...], out_ref[:WIDE, :WIDE])


def finish(at, prior, rhs, keys, panel, mine, across, first, inverse, pivot, solved):
    height, width = prior.shape
    blocks, samples, tall = keys.shape
    whole = lambda a: pl.BlockSpec(a.shape, lambda i: (0,) * a.ndim)
    return pl.pallas_call(
        finish_kernel,
        grid=(blocks,),
        in_specs=[
            pl.BlockSpec(memory_space=pltpu.SMEM),
            pl.BlockSpec((tall, width), lambda i: (i, 0)),
            pl.BlockSpec((tall, rhs.shape[1]), lambda i: (i, 0)),
            pl.BlockSpec((1, samples, tall), lambda i: (i, 0, 0)),
            pl.BlockSpec((1, WIDE, tall), lambda i: (i, 0, 0)),
            whole(mine),
            whole(across),
            whole(first),
            whole(inverse),
            whole(pivot),
            whole(solved),
        ],
        out_specs=[
            pl.BlockSpec((tall, width), lambda i: (i, 0)),
            pl.BlockSpec((tall, rhs.shape[1]), lambda i: (i, 0)),
        ],
        out_shape=[
            jax.ShapeDtypeStruct(prior.shape, jnp.float32),
            jax.ShapeDtypeStruct(rhs.shape, jnp.float32),
        ],
        compiler_params=pltpu.CompilerParams(
            dimension_semantics=("arbitrary",), vmem_limit_bytes=48 * 1024 * 1024
        ),
        name="finish",
    )(at, prior, rhs, keys, panel, mine, across, first, inverse, pivot, solved)


def mul(a, b, dims=NN):
    return lax.dot_general(a, b, dims, precision=HIGHEST, preferred_element_type=jnp.float32)


def factor(block):
    half = P_SIZE
    eye = jnp.eye(half, dtype=jnp.float32)
    first = lax.linalg.cholesky(block[:half, :half], symmetrize_input=False)
    first_inv = jax.scipy.linalg.solve_triangular(first, eye, lower=True)
    side = mul(block[half:, :half], first_inv, NT)
    second = lax.linalg.cholesky(block[half:, half:] - mul(side, side, NT), symmetrize_input=False)
    second_inv = jax.scipy.linalg.solve_triangular(second, eye, lower=True)
    side_inv = -mul(mul(second_inv, side), first_inv)
    none = jnp.zeros((half, half), jnp.float32)
    pivot = jnp.block([[first, none], [side, second]])
    inverse = jnp.block([[first_inv, none], [side_inv, second_inv]])
    return pivot, inverse


def local(hidden, w_gate, w_up, prior, rhs):
    row_id = lax.axis_index("row")
    col_id = lax.axis_index(COL)
    height, width = prior.shape

    tokens = copies(hidden, COL).reshape(-1, hidden.shape[1])
    samples = tokens.shape[0]

    top = row_tree(jnp.concatenate([prior[:WIDE], rhs[:WIDE]], axis=1))
    panel_cols, head = top[:, :width], top[:, width:]
    diagonal = col_tree(panel_cols[:, :WIDE])
    slab = WIDE // ROWS
    piece = lax.dynamic_slice_in_dim(panel_cols, row_id * slab, slab, 0).astype(jnp.float16)
    panel = gather_row_blocks(piece).reshape(YS, WIDE, width).astype(jnp.float32)

    gate_part = jnp.dot(tokens, w_gate, preferred_element_type=jnp.float32)
    up_part = jnp.dot(tokens, w_up, preferred_element_type=jnp.float32)
    parts = jnp.concatenate([gate_part, up_part], axis=1).reshape(ROWS, samples // ROWS, 2 * width)
    sums = lax.all_to_all(parts, "row", 0, 0, tiled=True).sum(0)
    mine = jax.nn.silu(sums[:, :width]) * sums[:, width:]

    keys_rows = gather_row_blocks(mine).reshape(YS, samples, width)
    keys_cols = copies(mine, "row").reshape(samples, width)
    first = col_tree(keys_cols[:, :WIDE])

    eye = jnp.eye(WIDE, dtype=jnp.float32)
    pivot, inverse = factor(diagonal + mul(first, first, TN) / samples + DAMP * eye)
    cross = panel_cols + mul(first, keys_cols, TN) / samples
    across = mul(inverse, cross)
    col_global = col_id * width + lax.iota(jnp.int32, width)
    line = lax.iota(jnp.int32, WIDE) // P_SIZE
    across = jnp.where(col_global[None, :] >= (line[:, None] + 1) * P_SIZE, across, 0.0)
    solved = mul(inverse, head)
    at = jnp.stack([row_id, col_id]).astype(jnp.int32)
    return finish(
        at, prior, rhs, keys_rows, panel, keys_cols, across, first, inverse, pivot, solved
    )


def solution(mesh):
    finer = Mesh(mesh.devices.reshape(ROWS, YS, ZS), ALL)
    return jax.shard_map(
        local,
        mesh=finer,
        in_specs=(P(COL, "row"), P("row", COL), P("row", COL), P("row", COL), P("row", COL)),
        out_specs=(P("row", COL), P("row", COL)),
        check_vma=False,
    )
```

time: 589 us -> 256 us (0.43)
  waiting for transfers between devices: 348 us -> 34.2 us
  starting transfers between devices: 14.5 us -> 93.7 us
  blocking collectives: 87.7 us -> 10.3 us
  matrix products: 33.2 us -> 17.7 us
  between operations: 14.5 us -> 1.08 us
  Pallas kernels: 0 us -> 13.2 us
  other arithmetic: 74.2 us -> 64.9 us
    psum x4 -> x0, waiting for transfers between devices: 258 us -> none  [spread(): shard = lax.psum(shard, axis)]
    ppermute x0 -> x15, starting transfers between devices: none -> 59 us  [the longest x10 41.5 us: col_tree(): got = lax.ppermute(x, COL, pairs)]
    all_gather x4 -> x0, blocking collectives: 51.6 us -> none  [broadcast(): lax.all_gather(shard, axis)]
    all_to_all x2 -> x1, blocking collectives: 36.1 us -> 10.3 us  [copies(): return lax.all_to_all(wide, axis, 0, 0, tiled=True)]
    all_gather x2 -> x0, waiting for transfers between devices: 25.4 us -> none  [broadcast(): lax.all_gather(shard, axis)]
    reduce_scatter x1 -> x0, waiting for transfers between devices: 24.4 us -> none  [side_by_side(): lax.psum_scatter(both, axis, scatter_dimension=dim, tiled=True)]
    all_to_all x2 -> x6, starting transfers between devices: 14.3 us -> 34.8 us  [the longest x5 30 us: copies(): return lax.all_to_all(wide, axis, 0, 0, tiled=True)]
    all_to_all x2 -> x6, waiting for transfers between devices: 40.4 us -> 21.4 us  [the longest x5 14.2 us: copies(): return lax.all_to_all(wide, axis, 0, 0, tiled=True)]
  transfers between devices with their start and end apart: 9 -> 21, of which waited for: 8 -> 6; matrix products, arithmetic and copies ran while one was open for 5% -> 36% of each run, Pallas kernels for 0% -> 0%
where the time goes in v1:
time: 256 us; the launch traced here: 254 us
  starting transfers between devices  93.7 us (37%)
  other arithmetic  64.9 us (25%)
  waiting for transfers between devices  34.2 us (13%)
  local copies, waits for them, and re-layouts  18.4 us (7%)
  matrix products  17.7 us (7%)
  Pallas kernels  13.2 us (5%)
  blocking collectives  10.3 us (4%)
    ppermute x10, starting transfers between devices, col_tree(): got = lax.ppermute(x, COL, pairs)  41.5 us
    all_to_all x5, starting transfers between devices, copies(): return lax.all_to_all(wide, axis, 0, 0, tiled=True)  30 us
    another operation x3, other arithmetic, factor(): lax.linalg.cholesky(block[half:, half:] - mul(side, side, NT), symmetrize...  14.8 us
    another operation x3, other arithmetic, factor(): first = lax.linalg.cholesky(block[:half, :half], symmetrize_input=False)  14.8 us
    all_to_all x5, waiting for transfers between devices, copies(): return lax.all_to_all(wide, axis, 0, 0, tiled=True)  14.2 us
    another operation x2, other arithmetic, factor(): second_inv = jax.scipy.linalg.solve_triangular(second, eye, lower=True)  13.6 us
    another operation x2, other arithmetic, factor(): first_inv = jax.scipy.linalg.solve_triangular(first, eye, lower=True)  13.5 us
    pallas_call x1, Pallas kernels, finish(): pl.pallas_call(finish_kernel, grid=(blocks,), in_specs=[pl.BlockSpec(memo...  13.2 us
  transfers between devices with their start and end apart: 21, of which 6 were waited for; matrix products, arithmetic and copies ran while one was open for 36% of the time, Pallas kernels for 0%

profile of v1, /device:TPU:4, one launch (start us, length us, event | category | flops | bytes accessed | tf_op | source)
XLA Modules:
  0.0 253.5 jit_solution(8364805131672166187)
XLA Ops:
  2.2 11.5 %all-to-all-start = ((bf16[32,4,1024]{2,1,0:T(4,128)(2,1)}), bf16[32,4,1024]{2,1,0:T(4,128)(2,1)S(1)}, u32[]{:S(2)}, u32[]{:S(2)}) async-start(bf16[32,4,1024]{2,1,0:T(4,128)(2,1)} %broadcast_in_dim.15), calls=%async_computation | async-start | bytes 524288 | tf_op jit(solution)/shard_map/all_to_all | solution.py:26
  17.1 9.1 %all-to-all-done = bf16[32,4,1024]{2,1,0:T(4,128)(2,1)S(1)} async-done(((bf16[32,4,1024]{2,1,0:T(4,128)(2,1)}), bf16[32,4,1024]{2,1,0:T(4,128)(2,1)S(1)}, u32[]{:S(2)}, u32[]{:S(2)}) %all-to-all-start) | async-done | bytes 262176 | tf_op jit(solution)/shard_map/all_to_all | solution.py:26
  35.5 4.8 %all-to-all-start.1 = ((f32[8,16,1024]{2,1,0:T(8,128)}), f32[8,16,1024]{2,1,0:T(8,128)S(1)}, u32[]{:S(2)}, u32[]{:S(2)}) async-start(f32[8,16,1024]{2,1,0:T(8,128)} %bitcast.2), calls=%async_computation.1 | async-start | bytes 1048576 | tf_op jit(solution)/shard_map/all_to_all | solution.py:194
  40.3 7.2 %all-to-all-done.1 = f32[8,16,1024]{2,1,0:T(8,128)S(1)} async-done(((f32[8,16,1024]{2,1,0:T(8,128)}), f32[8,16,1024]{2,1,0:T(8,128)S(1)}, u32[]{:S(2)}, u32[]{:S(2)}) %all-to-all-start.1) | async-done | bytes 524320 | tf_op jit(solution)/shard_map/all_to_all | solution.py:194
  49.6 10.3 %all_to_all.35 = f32[8,16,512]{2,1,0:T(8,128)S(1)} all-to-all(f32[8,16,512]{2,1,0:T(8,128)S(1)} %broadcast_in_dim.20), channel_id=1, replica_groups=mesh['row'=8,'col_0'=4,'col_1'=8] {'row'}, dimensions={0} | all-to-all | bytes 524288 | tf_op jit(solution)/shard_map/all_to_all | solution.py:26
  59.9 7.6 %collective-permute-start.10 = (f32[128,256]{1,0:T(8,128)S(1)}, f32[128,256]{1,0:T(8,128)S(1)}, u32[]{:S(2)}, u32[]{:S(2)}) collective-permute-start(f32[128,256]{1,0:T(8,128)S(1)} %slice.55), channel_id=1, source_target_pairs={{0,4},{32,36},{64,68},{96,100},{128,132},{160,164},{192,196},{224,... | collective-permute-start | bytes 393224 | tf_op jit(solution)/shard_map/ppermute | solution.py:42
  67.6 3.9 %collective-permute-start = (f32[16,512]{1,0:T(8,128)S(1)}, f32[16,512]{1,0:T(8,128)S(1)}, u32[]{:S(2)}, u32[]{:S(2)}) collective-permute-start(f32[16,512]{1,0:T(8,128)S(1)} %slice_multiply_fusion), channel_id=1, source_target_pairs={{0,0},{1,8},{2,16},{3,24},{4,32},{5,40},{6,48},{7,56},{8,64},{9,72... | collective-permute-start | bytes 98312 | tf_op jit(solution)/shard_map/ppermute | solution.py:56
  71.5 4.9 %collective-permute-start.11 = (f32[128,256]{1,0:T(8,128)S(1)}, f32[128,256]{1,0:T(8,128)}, u32[]{:S(2)}, u32[]{:S(2)}) collective-permute-start(f32[128,256]{1,0:T(8,128)S(1)} %broadcast_select_fusion.7), channel_id=1, source_target_pairs={{0,2},{4,6},{32,34},{36,38},{64,66},{68,70},{96,98},{100,102},{128... | collective-permute-start | bytes 393224 | tf_op jit(solution)/shard_map/ppermute | solution.py:42
  76.5 4.9 %collective-permute-start.5 = (f32[256,256]{1,0:T(8,128)S(1)}, f32[256,256]{1,0:T(8,128)}, u32[]{:S(2)}, u32[]{:S(2)}) collective-permute-start(f32[256,256]{1,0:T(8,128)S(1)} %slice.54), channel_id=1, source_target_pairs={{0,4},{32,36},{64,68},{96,100},{128,132},{160,164},{192,196},{224,... | collective-permute-start | bytes 786440 | tf_op jit(solution)/shard_map/ppermute | solution.py:42
  85.6 3.8 %collective-permute-start.12 = (f32[128,256]{1,0:T(8,128)S(1)}, f32[128,256]{1,0:T(8,128)S(1)}, u32[]{:S(2)}, u32[]{:S(2)}) collective-permute-start(f32[128,256]{1,0:T(8,128)S(1)} %broadcast_select_fusion.8), channel_id=1, source_target_pairs={{0,1},{2,3},{4,5},{6,7},{32,33},{34,35},{36,37},{38,39},{64,65},{6... | collective-permute-start | bytes 393224 | tf_op jit(solution)/shard_map/ppermute | solution.py:42
  89.6 5.0 %collective-permute-start.6 = (f32[256,256]{1,0:T(8,128)S(1)}, f32[256,256]{1,0:T(8,128)}, u32[]{:S(2)}, u32[]{:S(2)}) collective-permute-start(f32[256,256]{1,0:T(8,128)S(1)} %broadcast_select_fusion.3), channel_id=1, source_target_pairs={{0,2},{4,6},{32,34},{36,38},{64,66},{68,70},{96,98},{100,102},{128... | collective-permute-start | bytes 786440 | tf_op jit(solution)/shard_map/ppermute | solution.py:42
  94.6 8.3 %collective-permute-start.4 = (f16[32,512]{1,0:T(8,128)(2,1)S(1)}, f16[32,512]{1,0:T(8,128)(2,1)S(1)}, u32[]{:S(2)}, u32[]{:S(2)}) collective-permute-start(f16[32,512]{1,0:T(8,128)(2,1)S(1)} %dynamic-slice_convert_fusion), channel_id=1, source_target_pairs={{0,0},{1,8},{2,16},{3,24},{4,32},{5,40},{6,48},{7,56},{8,64},{9,72... | collective-permute-start | bytes 98312 | tf_op jit(solution)/shard_map/ppermute | solution.py:56
  105.2 6.2 %all-to-all-start.4 = ((f16[8,32,512]{2,1,0:T(8,128)(2,1)}), f16[8,32,512]{2,1,0:T(8,128)(2,1)S(1)}, u32[]{:S(2)}, u32[]{:S(2)}) async-start(f16[8,32,512]{2,1,0:T(8,128)(2,1)} %broadcast_in_dim.18), calls=%async_computation.4 | async-start | bytes 524288 | tf_op jit(solution)/shard_map/all_to_all | solution.py:26
  112.2 4.6 %collective-permute-start.7 = (f32[256,256]{1,0:T(8,128)}, f32[256,256]{1,0:T(8,128)}, u32[]{:S(2)}, u32[]{:S(2)}) collective-permute-start(f32[256,256]{1,0:T(8,128)} %broadcast_select_fusion.4), channel_id=1, source_target_pairs={{0,1},{2,3},{4,5},{6,7},{32,33},{34,35},{36,37},{38,39},{64,65},{6... | collective-permute-start | bytes 786440 | tf_op jit(solution)/shard_map/ppermute | solution.py:42
  118.8 5.1 %all-to-all-done.4 = f16[8,32,512]{2,1,0:T(8,128)(2,1)S(1)} async-done(((f16[8,32,512]{2,1,0:T(8,128)(2,1)}), f16[8,32,512]{2,1,0:T(8,128)(2,1)S(1)}, u32[]{:S(2)}, u32[]{:S(2)}) %all-to-all-start.4) | async-done | bytes 262176 | tf_op jit(solution)/shard_map/all_to_all | solution.py:26
  125.0 3.5 %all-to-all-start.5 = ((f16[4,8,32,512]{3,2,1,0:T(8,128)(2,1)}), f16[4,8,32,512]{3,2,1,0:T(8,128)(2,1)S(1)}, u32[]{:S(2)}, u32[]{:S(2)}) async-start(f16[4,8,32,512]{3,2,1,0:T(8,128)(2,1)} %broadcast_in_dim.19), calls=%async_computation.5 | async-start | bytes 2097152 | tf_op jit(solution)/shard_map/all_to_all | solution.py:26
  129.6 5.4 %collective-permute-start.8 = (f32[256,256]{1,0:T(8,128)S(1)}, f32[256,256]{1,0:T(8,128)S(1)}, u32[]{:S(2)}, u32[]{:S(2)}) collective-permute-start(f32[256,256]{1,0:T(8,128)S(1)} %broadcast_select_fusion.5), channel_id=1, source_target_pairs={{0,16},{1,17},{2,18},{3,19},{4,20},{5,21},{6,22},{7,23},{32,48},{3... | collective-permute-start | bytes 786440 | tf_op jit(solution)/shard_map/ppermute | solution.py:46
  136.4 9.2 %collective-permute-done.8 = f32[256,256]{1,0:T(8,128)S(1)} collective-permute-done((f32[256,256]{1,0:T(8,128)S(1)}, f32[256,256]{1,0:T(8,128)S(1)}, u32[]{:S(2)}, u32[]{:S(2)}) %collective-permute-start.8) | collective-permute-done | bytes 262176 | tf_op jit(solution)/shard_map/ppermute | solution.py:46
  149.7 5.3 %all-to-all-start.3 = ((f32[4,8,16,512]{3,2,1,0:T(8,128)}), f32[4,8,16,512]{3,2,1,0:T(8,128)}, u32[]{:S(2)}, u32[]{:S(2)}) async-start(f32[4,8,16,512]{3,2,1,0:T(8,128)} %broadcast_in_dim.17), calls=%async_computation.3 | async-start | bytes 2097152 | tf_op jit(solution)/shard_map/all_to_all | solution.py:26
  159.3 13.2 %custom-call.8 = f32[128,128]{1,0:T(8,128)} custom-call(f32[128,128]{1,0:T(8,128)} %slice.56), custom_call_target="Cholesky" | custom-call | tf_op jit(solution)/shard_map/cholesky/custom-call.1 | solution.py:164
  176.3 11.3 %custom-call.9 = f32[1,128,128]{1,2,0:T(8,128)} custom-call(f32[1,128,128]{2,1,0:T(8,128)} %get-tuple-element.6), custom_call_target="InvertDiagBlocksLowerTriangular" | custom-call | tf_op jit(solution)/shard_map/jit(_solve_triangular)/triangular_solve | solution.py:165
  192.8 13.2 %custom-call.10 = f32[128,128]{1,0:T(8,128)} custom-call(f32[128,128]{1,0:T(8,128)} %slice_subtract_fusion), custom_call_target="Cholesky" | custom-call | tf_op jit(solution)/shard_map/cholesky/custom-call.1 | solution.py:167
  209.7 11.4 %custom-call.11 = f32[1,128,128]{1,2,0:T(8,128)} custom-call(f32[1,128,128]{2,1,0:T(8,128)} %get-tuple-element.4), custom_call_target="InvertDiagBlocksLowerTriangular" | custom-call | tf_op jit(solution)/shard_map/jit(_solve_triangular)/triangular_solve | solution.py:168
  240.3 13.2 %finish.1 = (f32[2048,512]{1,0:T(8,128)}, f32[2048,128]{1,0:T(8,128)}) custom-call(s32[2]{0:T(128)S(1)} %pad_add_fusion.at_ref, f32[2048,512]{1,0:T(8,128)} %prior_ref.1, f32[2048,128]{1,0:T(8,128)S(1)} %copy-done.2, f32[4,128,512]{2,1,0:T(8,128)} %bitcast.3.keys_ref, f32[4,256,512]{2,1,0:T(8,128)S(1)} %bitcast_convert_fusion.panel_ref, ...), custom_call_target="tpu_custom_call" | custom-call | tf_op jit(solution)/shard_map/finish/pallas_call | solution.py:126
  (101 shorter events, 69.5 us)
Async XLA Ops:
  0.6 25.6 %copy-start = (bf16[1024,512]{1,0:T(8,128)(2,1)S(1)}, bf16[1024,512]{1,0:T(8,128)(2,1)}, u32[]{:S(2)}) copy-start(bf16[1024,512]{1,0:T(8,128)(2,1)} %param.10) | copy-start | bytes 3145732
  2.2 23.9 %all-to-all-start = ((bf16[32,4,1024]{2,1,0:T(4,128)(2,1)}), bf16[32,4,1024]{2,1,0:T(4,128)(2,1)S(1)}, u32[]{:S(2)}, u32[]{:S(2)}) async-start(bf16[32,4,1024]{2,1,0:T(4,128)(2,1)} %broadcast_in_dim.15), calls=%async_computation | async-start | bytes 524288 | tf_op jit(solution)/shard_map/all_to_all | solution.py:26
  15.8 14.1 %collective-permute-start.1 = (f32[256,640]{1,0:T(8,128)S(1)}, f32[256,640]{1,0:T(8,128)}, u32[]{:S(2)}, u32[]{:S(2)}) collective-permute-start(f32[256,640]{1,0:T(8,128)S(1)} %pad_maximum_fusion), channel_id=1, source_target_pairs={{0,128},{1,129},{2,130},{3,131},{4,132},{5,133},{6,134},{7,135},{8... | collective-permute-start | bytes 1966088 | tf_op jit(solution)/shard_map/ppermute | solution.py:33
  31.0 16.5 %collective-permute-start.2 = (f32[256,640]{1,0:T(8,128)S(1)}, f32[256,640]{1,0:T(8,128)}, u32[]{:S(2)}, u32[]{:S(2)}) collective-permute-start(f32[256,640]{1,0:T(8,128)S(1)} %broadcast_select_fusion), channel_id=1, source_target_pairs={{0,64},{128,192},{1,65},{129,193},{2,66},{130,194},{3,67},{131,195... | collective-permute-start | bytes 1966088 | tf_op jit(solution)/shard_map/ppermute | solution.py:33
  35.5 12.0 %all-to-all-start.1 = ((f32[8,16,1024]{2,1,0:T(8,128)}), f32[8,16,1024]{2,1,0:T(8,128)S(1)}, u32[]{:S(2)}, u32[]{:S(2)}) async-start(f32[8,16,1024]{2,1,0:T(8,128)} %bitcast.2), calls=%async_computation.1 | async-start | bytes 1048576 | tf_op jit(solution)/shard_map/all_to_all | solution.py:194
  47.7 28.8 %collective-permute-start.3 = (f32[256,640]{1,0:T(8,128)S(1)}, f32[256,640]{1,0:T(8,128)S(1)}, u32[]{:S(2)}, u32[]{:S(2)}) collective-permute-start(f32[256,640]{1,0:T(8,128)S(1)} %broadcast_select_fusion.1), channel_id=1, source_target_pairs={{0,32},{64,96},{128,160},{192,224},{1,33},{65,97},{129,161},{193,2... | collective-permute-start | bytes 1966088 | tf_op jit(solution)/shard_map/ppermute | solution.py:33
  59.9 11.6 %collective-permute-start.10 = (f32[128,256]{1,0:T(8,128)S(1)}, f32[128,256]{1,0:T(8,128)S(1)}, u32[]{:S(2)}, u32[]{:S(2)}) collective-permute-start(f32[128,256]{1,0:T(8,128)S(1)} %slice.55), channel_id=1, source_target_pairs={{0,4},{32,36},{64,68},{96,100},{128,132},{160,164},{192,196},{224,... | collective-permute-start | bytes 393224 | tf_op jit(solution)/shard_map/ppermute | solution.py:42
  67.6 13.9 %collective-permute-start = (f32[16,512]{1,0:T(8,128)S(1)}, f32[16,512]{1,0:T(8,128)S(1)}, u32[]{:S(2)}, u32[]{:S(2)}) collective-permute-start(f32[16,512]{1,0:T(8,128)S(1)} %slice_multiply_fusion), channel_id=1, source_target_pairs={{0,0},{1,8},{2,16},{3,24},{4,32},{5,40},{6,48},{7,56},{8,64},{9,72... | collective-permute-start | bytes 98312 | tf_op jit(solution)/shard_map/ppermute | solution.py:56
  71.5 14.1 %collective-permute-start.11 = (f32[128,256]{1,0:T(8,128)S(1)}, f32[128,256]{1,0:T(8,128)}, u32[]{:S(2)}, u32[]{:S(2)}) collective-permute-start(f32[128,256]{1,0:T(8,128)S(1)} %broadcast_select_fusion.7), channel_id=1, source_target_pairs={{0,2},{4,6},{32,34},{36,38},{64,66},{68,70},{96,98},{100,102},{128... | collective-permute-start | bytes 393224 | tf_op jit(solution)/shard_map/ppermute | solution.py:42
  76.5 58.5 %copy-start.6 = (f32[256,640]{1,0:T(8,128)}, f32[256,640]{1,0:T(8,128)S(1)}, u32[]{:S(2)}) copy-start(f32[256,640]{1,0:T(8,128)S(1)} %broadcast_select_fusion.2) | copy-start | bytes 1966084
  76.5 13.0 %collective-permute-start.5 = (f32[256,256]{1,0:T(8,128)S(1)}, f32[256,256]{1,0:T(8,128)}, u32[]{:S(2)}, u32[]{:S(2)}) collective-permute-start(f32[256,256]{1,0:T(8,128)S(1)} %slice.54), channel_id=1, source_target_pairs={{0,4},{32,36},{64,68},{96,100},{128,132},{160,164},{192,196},{224,... | collective-permute-start | bytes 786440 | tf_op jit(solution)/shard_map/ppermute | solution.py:42
  82.2 22.0 %all-to-all-start.2 = ((f32[8,16,512]{2,1,0:T(8,128)}), f32[8,16,512]{2,1,0:T(8,128)S(1)}, u32[]{:S(2)}, u32[]{:S(2)}) async-start(f32[8,16,512]{2,1,0:T(8,128)} %broadcast_in_dim.16), calls=%async_computation.2 | async-start | bytes 524288 | tf_op jit(solution)/shard_map/all_to_all | solution.py:26
  85.6 17.2 %collective-permute-start.12 = (f32[128,256]{1,0:T(8,128)S(1)}, f32[128,256]{1,0:T(8,128)S(1)}, u32[]{:S(2)}, u32[]{:S(2)}) collective-permute-start(f32[128,256]{1,0:T(8,128)S(1)} %broadcast_select_fusion.8), channel_id=1, source_target_pairs={{0,1},{2,3},{4,5},{6,7},{32,33},{34,35},{36,37},{38,39},{64,65},{6... | collective-permute-start | bytes 393224 | tf_op jit(solution)/shard_map/ppermute | solution.py:42
  89.6 21.8 %collective-permute-start.6 = (f32[256,256]{1,0:T(8,128)S(1)}, f32[256,256]{1,0:T(8,128)}, u32[]{:S(2)}, u32[]{:S(2)}) collective-permute-start(f32[256,256]{1,0:T(8,128)S(1)} %broadcast_select_fusion.3), channel_id=1, source_target_pairs={{0,2},{4,6},{32,34},{36,38},{64,66},{68,70},{96,98},{100,102},{128... | collective-permute-start | bytes 786440 | tf_op jit(solution)/shard_map/ppermute | solution.py:42
  94.6 9.9 %collective-permute-start.4 = (f16[32,512]{1,0:T(8,128)(2,1)S(1)}, f16[32,512]{1,0:T(8,128)(2,1)S(1)}, u32[]{:S(2)}, u32[]{:S(2)}) collective-permute-start(f16[32,512]{1,0:T(8,128)(2,1)S(1)} %dynamic-slice_convert_fusion), channel_id=1, source_target_pairs={{0,0},{1,8},{2,16},{3,24},{4,32},{5,40},{6,48},{7,56},{8,64},{9,72... | collective-permute-start | bytes 98312 | tf_op jit(solution)/shard_map/ppermute | solution.py:56
  102.9 13.9 %collective-permute-start.13 = (f32[128,256]{1,0:T(8,128)S(1)}, f32[128,256]{1,0:T(8,128)S(1)}, u32[]{:S(2)}, u32[]{:S(2)}) collective-permute-start(f32[128,256]{1,0:T(8,128)S(1)} %broadcast_select_fusion.9), channel_id=1, source_target_pairs={{0,16},{1,17},{2,18},{3,19},{4,20},{5,21},{6,22},{7,23},{32,48},{3... | collective-permute-start | bytes 393224 | tf_op jit(solution)/shard_map/ppermute | solution.py:46
  105.2 18.7 %all-to-all-start.4 = ((f16[8,32,512]{2,1,0:T(8,128)(2,1)}), f16[8,32,512]{2,1,0:T(8,128)(2,1)S(1)}, u32[]{:S(2)}, u32[]{:S(2)}) async-start(f16[8,32,512]{2,1,0:T(8,128)(2,1)} %broadcast_in_dim.18), calls=%async_computation.4 | async-start | bytes 524288 | tf_op jit(solution)/shard_map/all_to_all | solution.py:26
  112.2 16.4 %collective-permute-start.7 = (f32[256,256]{1,0:T(8,128)}, f32[256,256]{1,0:T(8,128)}, u32[]{:S(2)}, u32[]{:S(2)}) collective-permute-start(f32[256,256]{1,0:T(8,128)} %broadcast_select_fusion.4), channel_id=1, source_target_pairs={{0,1},{2,3},{4,5},{6,7},{32,33},{34,35},{36,37},{38,39},{64,65},{6... | collective-permute-start | bytes 786440 | tf_op jit(solution)/shard_map/ppermute | solution.py:42
  116.9 18.1 %collective-permute-start.14 = (f32[128,256]{1,0:T(8,128)S(1)}, f32[128,256]{1,0:T(8,128)}, u32[]{:S(2)}, u32[]{:S(2)}) collective-permute-start(f32[128,256]{1,0:T(8,128)S(1)} %broadcast_select_fusion.10), channel_id=1, source_target_pairs={{0,8},{1,9},{2,10},{3,11},{4,12},{5,13},{6,14},{7,15},{16,24},{17,... | collective-permute-start | bytes 393224 | tf_op jit(solution)/shard_map/ppermute | solution.py:46
  125.0 23.4 %all-to-all-start.5 = ((f16[4,8,32,512]{3,2,1,0:T(8,128)(2,1)}), f16[4,8,32,512]{3,2,1,0:T(8,128)(2,1)S(1)}, u32[]{:S(2)}, u32[]{:S(2)}) async-start(f16[4,8,32,512]{3,2,1,0:T(8,128)(2,1)} %broadcast_in_dim.19), calls=%async_computation.5 | async-start | bytes 2097152 | tf_op jit(solution)/shard_map/all_to_all | solution.py:26
  129.6 16.1 %collective-permute-start.8 = (f32[256,256]{1,0:T(8,128)S(1)}, f32[256,256]{1,0:T(8,128)S(1)}, u32[]{:S(2)}, u32[]{:S(2)}) collective-permute-start(f32[256,256]{1,0:T(8,128)S(1)} %broadcast_select_fusion.5), channel_id=1, source_target_pairs={{0,16},{1,17},{2,18},{3,19},{4,20},{5,21},{6,22},{7,23},{32,48},{3... | collective-permute-start | bytes 786440 | tf_op jit(solution)/shard_map/ppermute | solution.py:46
  146.4 10.2 %collective-permute-start.9 = (f32[256,256]{1,0:T(8,128)}, f32[256,256]{1,0:T(8,128)}, u32[]{:S(2)}, u32[]{:S(2)}) collective-permute-start(f32[256,256]{1,0:T(8,128)} %broadcast_select_fusion.6), channel_id=1, source_target_pairs={{0,8},{1,9},{2,10},{3,11},{4,12},{5,13},{6,14},{7,15},{16,24},{17,... | collective-permute-start | bytes 786440 | tf_op jit(solution)/shard_map/ppermute | solution.py:46
  148.4 1.3 copy-start.7
  149.7 85.5 %all-to-all-start.3 = ((f32[4,8,16,512]{3,2,1,0:T(8,128)}), f32[4,8,16,512]{3,2,1,0:T(8,128)}, u32[]{:S(2)}, u32[]{:S(2)}) async-start(f32[4,8,16,512]{3,2,1,0:T(8,128)} %broadcast_in_dim.17), calls=%async_computation.3 | async-start | bytes 2097152 | tf_op jit(solution)/shard_map/all_to_all | solution.py:26
  (8 other events, 7.0 us)
